TPU v7x, 32 devices: a whole 2x2x4 slice. The times are simulated.
32 devices in a mesh: rep: 16 (over z, x, core), fsdp: 2 (over y).
Axes of the slice: x: 2, y: 2, z: 4, core: 2. Of those that a mesh axis runs over, the one named last changes fastest.
Arguments:
- gradients: bfloat16 [16, 4, 64, 4096], P('rep', None, 'fsdp'), may hold values from -8000 to 8000
- local_params: float32 [16, 4, 64, 4096], P('rep', None, 'fsdp'), may hold values from -6 to 6
- first_moment: float32 [16, 4, 64, 4096], P('rep', None, 'fsdp'), may hold values from -6 to 6
- second_moment: float32 [16, 4, 64, 4096], P('rep', None, 'fsdp'), may hold values from 0.05 to 2
- global_params: float32 [4, 64, 4096], P(None, 'fsdp'), may hold values from -6 to 6
- outer_momentum: float32 [4, 64, 4096], P(None, 'fsdp'), may hold values from -6 to 6
Outputs:
- new_global: float32 [4, 64, 4096], P(None, 'fsdp')
- new_momentum: float32 [4, 64, 4096], P(None, 'fsdp')
- new_first: float32 [16, 4, 64, 4096], P('rep', None, 'fsdp')
- new_second: float32 [16, 4, 64, 4096], P('rep', None, 'fsdp')
All inputs are finite; a program needn't handle non-finite values.
Results may differ from a plain program's by a relative error of at most 0.0003.
Values sent between devices are 32-bit elements; how exact they have to be, the bound alone decides.
A program may use at most 128 MiB of HBM per device.

v0:
```python
import jax
import jax.numpy as jnp
from jax import lax
from jax.sharding import PartitionSpec as P

STEP = 20


def outer_step(delta, global_now, momentum_now, replicas):
    pseudo = lax.psum(delta, "rep") / replicas
    momentum_next = 0.9 * momentum_now + pseudo
    global_next = global_now - 0.7 * (pseudo + 0.9 * momentum_next)
    return (global_next, momentum_next)


def on_device(gradients, local_params, first_moment, second_moment, global_params, outer_momentum):
    first_fix = 1.0 - 0.9**STEP
    second_fix = 1.0 - 0.95**STEP
    gradient = gradients[0].astype(jnp.float32)
    squares = lax.psum(jnp.sum(gradient * gradient), "fsdp")
    count_all = gradient.size * lax.axis_size("fsdp")
    factor = jnp.minimum(1.0, 0.5 / jnp.sqrt(squares / count_all))
    replicas = lax.axis_size("rep")
    firsts, seconds, deltas, globals_new, momenta_new = ([], [], [], [], [])
    for matrix in range(gradient.shape[0]):
        clipped = gradient[matrix] * factor
        first_new = 0.9 * first_moment[0, matrix] + 0.1 * clipped
        second_new = 0.95 * second_moment[0, matrix] + 0.05 * clipped * clipped
        update = first_new / first_fix / (jnp.sqrt(second_new / second_fix) + 1e-08)
        local_now = local_params[0, matrix]
        stepped = local_now - 0.1 * (update + 0.1 * local_now)
        delta = global_params[matrix] - stepped
        first_new, second_new, delta = (first_new, second_new, delta)
        firsts.append(first_new)
        seconds.append(second_new)
        global_next, momentum_next = outer_step(
            delta[None],
            global_params[matrix : matrix + 1],
            outer_momentum[matrix : matrix + 1],
            replicas,
        )
        globals_new.append(global_next)
        momenta_new.append(momentum_next)
    global_all = jnp.concatenate(globals_new, axis=0)
    momentum_all = jnp.concatenate(momenta_new, axis=0)
    return (global_all, momentum_all, jnp.stack(firsts)[None], jnp.stack(seconds)[None])


def solution(mesh):
    placed = (
        P("rep", None, "fsdp", None),
        P("rep", None, "fsdp", None),
        P("rep", None, "fsdp", None),
        P("rep", None, "fsdp", None),
        P(None, "fsdp", None),
        P(None, "fsdp", None),
    )
    return jax.shard_map(
        on_device,
        mesh=mesh,
        in_specs=placed,
        out_specs=(
            P(None, "fsdp", None),
            P(None, "fsdp", None),
            P("rep", None, "fsdp", None),
            P("rep", None, "fsdp", None),
        ),
        check_vma=False,
    )
```

profile of v0, /device:TPU:1, one launch (start us, length us, event | category | flops | bytes accessed | tf_op | source)
XLA Modules:
  0.0 138.0 jit_solution(10752124649814436725)
XLA Ops:
  7.2 0.0 copy-start
  7.2 0.0 all-reduce.3.cloned.1.call-start
  7.2 2.5 %multiply_reduce_fusion = f32[]{:T(128)} fusion(bf16[1,4,32,4096]{3,2,1,0:T(8,128)(2,1)} %param.6), kind=kLoop, calls=%fused_computation.4 | loop fusion | flops 1572863 | bytes 1048580 | tf_op jit(solution)/shard_map/reduce_sum | solution.py:20
  9.7 2.8 %convert_element_type.4 = f32[1,4,32,4096]{3,2,1,0:T(8,128)} convert(bf16[1,4,32,4096]{3,2,1,0:T(8,128)(2,1)} %param.6) | non-fusion elementwise | flops 524288 | bytes 3145728 | tf_op jit(solution)/shard_map/convert_element_type | solution.py:19
  12.5 5.0 %psum.35 = f32[]{:T(128)} all-reduce(f32[]{:T(128)} %multiply_reduce_fusion), channel_id=1, replica_groups=mesh['rep'=16,'fsdp'=2] {'fsdp'}, use_global_device_ids=true, to_apply=%region_1.0 | all-reduce | flops 1 | bytes 8 | tf_op jit(solution)/shard_map/psum | solution.py:20
  18.2 0.0 copy-done
  18.2 0.0 copy-start.1
  18.2 0.0 copy-start.2
  18.2 2.9 %fusion.13 = (f32[1,32,4096]{2,1,0:T(8,128)}, f32[1,32,4096]{2,1,0:T(8,128)S(1)}, f32[1,32,4096]{2,1,0:T(8,128)S(1)}) fusion(f32[1,4,32,4096]{3,2,1,0:T(8,128)} %param.7, f32[4,32,4096]{2,1,0:T(8,128)S(1)} %copy-done, f32[]{:T(128)S(6)} %min_shard_map.3, f32[1,4,32,4096]{3,2,1,0:T(8,128)} %convert_element_type.4, f32[1,4,32,4096]{3,2,1,0:T(8,128)} %param.8, ...), kind=kLoop, calls=%fused_computation.32 | loop fusion | flops 2228224 | bytes 4194308 | tf_op jit(solution)/shard_map/sub | solution.py:32
  21.1 0.0 copy-done.1
  21.1 0.0 copy-done.2
  21.1 4.5 %fusion.19 = (f32[1,32,4096]{2,1,0:T(8,128)}, f32[1,32,4096]{2,1,0:T(8,128)}, f32[1,32,4096]{2,1,0:T(8,128)}, f32[1,32,4096]{2,1,0:T(8,128)}, f32[1,32,4096]{2,1...) fusion(f32[1,4,32,4096]{3,2,1,0:T(8,128)S(1)} %copy-done.2, ...), kind=kLoop, calls=%fused_computation.44 | loop fusion | flops 6684672 | bytes 12582916 | tf_op jit(solution)/shard_map/sub | solution.py:32
  25.6 0.0 all-reduce.3.cloned.1.call-update
  25.7 4.2 %maximum_bitcast_fusion = (f32[1,4,32,4096]{3,2,1,0:T(8,128)}, f32[1,4,32,4096]{3,2,1,0:T(8,128)}) fusion(f32[1,32,4096]{2,1,0:T(8,128)} %get-tuple-element.25, f32[1,32,4096]{2,1,0:T(8,128)S(1)} %get-tuple-element.15, f32[1,32,4096]{2,1,0:T(8,128)} %get-tuple-element.22, f32[1,32,4096]{2,1,0:T(8,128)} %get-tuple-element.9, ...), kind=kLoop, calls=%fused_computation.2 | loop fusion | flops 3145728 | bytes 8388608 | tf_op jit(solution)/shard_map/broadcast_in_dim | solution.py:46
  29.9 96.1 %all-reduce.3.cloned.1.call-done = (f32[1,32,4096]{2,1,0:T(8,128)}, f32[1,32,4096]{2,1,0:T(8,128)}, f32[1,32,4096]{2,1,0:T(8,128)}, f32[1,32,4096]{2,1,0:T(8,128)}) async-done(((f32[1,32,4096]{2,1,0:T(8,128)}, f32[1,32,4096]{2,1,0:T(8,128)}, f32[1,32,4096]{2,1,0:T(8,128)}, f32[1,32,4096]{2,1,0:T(8,128)}), (f32[1,32,4096]{2,1,0:T(8,128)}, f32[1,32,4096]{2,1,0:T(8,128)}, f32[1,32,4096]{2,1,0:T(8,128)}, ...) | async-done | bytes 2097168 | tf_op jit(solution)/shard_map/psum | solution.py:10
  126.0 2.7 %multiply_subtract_fusion.3 = (f32[1,32,4096]{2,1,0:T(8,128)S(1)}, f32[1,32,4096]{2,1,0:T(8,128)S(1)}, f32[1,32,4096]{2,1,0:T(8,128)S(1)}, f32[1,32,4096]{2,1,0:...) fusion(f32[1,32,4096]{2,1,0:T(8,128)} %get-tuple-element.7, ...), kind=kLoop, calls=%fused_computation.51 | loop fusion | flops 3670016 | bytes 10485760 | tf_op jit(solution)/shard_map/sub | solution.py:12
  128.7 2.5 %pad_maximum_fusion = (f32[4,32,4096]{2,1,0:T(8,128)}, f32[4,32,4096]{2,1,0:T(8,128)}) fusion(f32[1,32,4096]{2,1,0:T(8,128)S(1)} %get-tuple-element.29, f32[1,32,4096]{2,1,0:T(8,128)S(1)} %get-tuple-element.28, f32[1,32,4096]{2,1,0:T(8,128)S(1)} %get-tuple-element.27, f32[1,32,4096]{2,1,0:T(8,128)S(1)} %get-tuple-element.26, ...), kind=kLoop, calls=%fused_computation | loop fusion | flops 3145728 | bytes 8388608 | tf_op jit(solution)/shard_map/concatenate | solution.py:44
Async XLA Ops:
  7.2 11.0 %copy-start = (f32[4,32,4096]{2,1,0:T(8,128)S(1)}, f32[4,32,4096]{2,1,0:T(8,128)}, u32[]{:S(2)}) copy-start(f32[4,32,4096]{2,1,0:T(8,128)} %param.10) | copy-start | bytes 6291460
  7.2 118.8 %all-reduce.3.cloned.1.call-start = ((), (), s32[]{:S(2)}) async-start(), calls=%async_computation | async-start | bytes 4194304 | tf_op jit(solution)/shard_map/psum | solution.py:10
  18.2 2.9 %copy-start.1 = (f32[1,4,32,4096]{3,2,1,0:T(8,128)S(1)}, f32[1,4,32,4096]{3,2,1,0:T(8,128)}, u32[]{:S(2)}) copy-start(f32[1,4,32,4096]{3,2,1,0:T(8,128)} %convert_element_type.4) | copy-start | bytes 6291460
  18.2 2.9 %copy-start.2 = (f32[1,4,32,4096]{3,2,1,0:T(8,128)S(1)}, f32[1,4,32,4096]{3,2,1,0:T(8,128)}, u32[]{:S(2)}) copy-start(f32[1,4,32,4096]{3,2,1,0:T(8,128)} %param.7) | copy-start | bytes 6291460
Sparse Core Ops, SparseCore 0:
  25.8 100.1 all-reduce.2
where the time goes:
time: 140 us; the launch traced here: 138 us
  waiting for transfers between devices  96.1 us (69%)
  other arithmetic  22.2 us (16%)
  between operations  14.8 us (11%)
  blocking collectives  4.98 us (4%)
    psum x1, waiting for transfers between devices, outer_step(): pseudo = lax.psum(delta, 'rep') / replicas  96.1 us
    sub x2, other arithmetic, on_device(): delta = global_params[matrix] - stepped  7.45 us
    psum x1, blocking collectives, on_device(): squares = lax.psum(jnp.sum(gradient * gradient), 'fsdp')  4.98 us
    broadcast_in_dim x1, other arithmetic, on_device(): jnp.stack(firsts)[None]  4.24 us
  transfers between devices with their start and end apart: 1, of which 1 were waited for; matrix products, arithmetic and copies ran while one was open for 3% of the time, Pallas kernels for 0%

commit v1 on v0

v1 whole, which is shorter than its diff:
```python
import functools

import jax
import jax.numpy as jnp
from jax import lax
from jax.experimental import pallas as pl
from jax.experimental.pallas import tpu as pltpu
from jax.sharding import PartitionSpec as P

STEP = 20
FIRST_FIX = 1.0 - 0.9**STEP
SECOND_FIX = 1.0 - 0.95**STEP
CHUNKS = 4
MESH = pl.DeviceIdType.MESH


def kernel(shape, g_hbm, p_hbm, f_hbm, s_hbm, mean_hbm, factor_ref,
           g, p, f, s, delta, recv_c, part_x, recv_x, part_z, recv_z, res, squares,
           load_sem, sq_send, sq_recv, c_send, c_recv, x_send, x_recv, z_send, z_recv,
           gz_send, gz_recv, gx_send, gx_recv, gc_send, gc_recv, out_sem):
    reps, peers, depth = shape
    rows, width = delta.shape[3], delta.shape[4]
    chunks = delta.shape[0]
    me = lax.axis_index("rep")
    fs = lax.axis_index("fsdp")
    core = lax.rem(me, 2)
    x = lax.rem(me // 2, 2)
    z = me // 4
    mine = 2 * core + x
    other_core = {"rep": me + 1 - 2 * core}
    other_x = {"rep": me + 2 - 4 * x}

    def along_z(d):
        return {"rep": lax.rem(z + d, depth) * 4 + mine_id}

    mine_id = lax.rem(me, 4)

    loads = [pltpu.make_async_copy(src, dst, load_sem.at[i])
             for i, (src, dst) in enumerate(((g_hbm, g), (f_hbm, f), (s_hbm, s), (p_hbm, p)))]
    for load in loads:
        load.start()

    barrier = pltpu.get_barrier_semaphore()
    pl.semaphore_signal(barrier, inc=1, device_id=other_core, device_id_type=MESH)
    pl.semaphore_signal(barrier, inc=1, device_id=other_x, device_id_type=MESH)
    for d in range(1, depth):
        pl.semaphore_signal(barrier, inc=1, device_id=along_z(d), device_id_type=MESH)
    for d in range(1, peers):
        pl.semaphore_signal(barrier, inc=1, device_id={"fsdp": lax.rem(fs + d, peers)}, device_id_type=MESH)

    loads[0].wait()
    step = 512
    per = g.shape[2] // step

    def square(i, acc):
        part = g[i // per, :, pl.ds(pl.multiple_of(lax.rem(i, per) * step, step), step)].astype(jnp.float32)
        return acc + part * part

    acc = lax.fori_loop(0, g.shape[0] * per, square, jnp.zeros((rows, step), jnp.float32))
    acc = sum(acc[:, i * 128:(i + 1) * 128] for i in range(step // 128))
    squares[0] = sum(acc[i * 8:(i + 1) * 8] for i in range(rows // 8))

    pl.semaphore_wait(barrier, 2 + depth - 1 + peers - 1)
    sq = []
    for d in range(1, peers):
        copy = pltpu.make_async_remote_copy(
            squares.at[0], squares.at[d], sq_send.at[d], sq_recv.at[d],
            device_id={"fsdp": lax.rem(fs + d, peers)}, device_id_type=MESH)
        copy.start()
        sq.append(copy)
    for copy in sq:
        copy.wait()
    total = squares[0]
    for d in range(1, peers):
        total = total + squares[d]
    mean_sq = jnp.sum(total, keepdims=True) / (g.shape[0] * rows * g.shape[2] * peers)
    factor = jnp.where(mean_sq > 0.25, 0.5 / jnp.sqrt(mean_sq), 1.0)
    factor_ref[...] = jnp.broadcast_to(factor, factor_ref.shape)
    for load in loads[1:]:
        load.wait()

    def columns(k, zz):
        return pl.ds(pl.multiple_of((k * depth + zz) * width, width), width)

    def half(k, which):
        def piece(i, _):
            m = 2 * which + i // depth
            zz = lax.rem(i, depth)
            at = columns(k, zz)
            clipped = g[m, :, at].astype(jnp.float32) * factor
            first = 0.9 * f[m, :, at] + 0.1 * clipped
            second = 0.95 * s[m, :, at] + 0.05 * clipped * clipped
            update = (first * (0.1 / FIRST_FIX)) / (jnp.sqrt(second * (1.0 / SECOND_FIX)) + 1e-8)
            delta[k, m, zz] = 0.99 * p[m, :, at] - update
            return 0
        lax.fori_loop(0, 2 * depth, piece, 0)

    def remote(src, dst, send, recv, where):
        return pltpu.make_async_remote_copy(src, dst, send, recv, device_id=where, device_id_type=MESH)

    def c_copy(k):
        return remote(delta.at[k, pl.ds(2 * (1 - core), 2)], recv_c.at[k], c_send.at[k], c_recv.at[k], other_core)

    def x_copy(k):
        return remote(part_x.at[k], recv_x.at[k], x_send.at[k], x_recv.at[k], other_x)

    def z_copy(k, d):
        return remote(part_z.at[k, lax.rem(z + d, depth)], recv_z.at[k, d], z_send.at[k, d], z_recv.at[k, d], along_z(d))

    def gz_copy(k, d):
        return remote(res.at[k, mine, z], res.at[k, mine, z], gz_send.at[k, d], gz_recv.at[k, d], along_z(d))

    def gx_copy(k):
        return remote(res.at[k, mine], res.at[k, mine], gx_send.at[k], gx_recv.at[k], other_x)

    def gc_copy(k):
        own = res.at[k, pl.ds(2 * core, 2)]
        return remote(own, own, gc_send.at[k], gc_recv.at[k], other_core)

    def out_copy(k, m, zz):
        return pltpu.make_async_copy(res.at[k, m, zz], mean_hbm.at[m, :, columns(k, zz)], out_sem.at[k, m, zz])

    def compute(k):
        half(k, 1 - core)
        c_copy(k).start()
        half(k, core)

    def reduce_core(k):
        c_copy(k).wait_recv()

        def piece(i, _):
            part_x[k, i] = delta[k, 2 * core + 1 - x, i] + recv_c[k, 1 - x, i]
            return 0
        lax.fori_loop(0, depth, piece, 0)
        x_copy(k).start()

    def reduce_x(k):
        x_copy(k).wait_recv()

        def piece(i, _):
            part_z[k, i] = delta[k, mine, i] + recv_c[k, x, i] + recv_x[k, i]
            return 0
        lax.fori_loop(0, depth, piece, 0)
        for d in range(1, depth):
            z_copy(k, d).start()

    def reduce_z(k):
        for d in range(1, depth):
            z_copy(k, d).wait_recv()
        total = part_z[k, z]
        for d in range(1, depth):
            total = total + recv_z[k, d]
        res[k, mine, z] = total * (1.0 / reps)
        for d in range(1, depth):
            gz_copy(k, d).start()

    def gather_z(k):
        for d in range(1, depth):
            gz_copy(k, d).wait_recv()
        gx_copy(k).start()

    def gather_x(k):
        gx_copy(k).wait_recv()
        gc_copy(k).start()

    def gather_core(k):
        gc_copy(k).wait_recv()
        for m in range(4):
            for zz in range(depth):
                out_copy(k, m, zz).start()

    for k in range(chunks):
        compute(k)
        if k:
            reduce_core(k - 1)
    reduce_core(chunks - 1)
    stages = (reduce_x, reduce_z, gather_z, gather_x, gather_core)
    for t in range(chunks + len(stages) - 1):
        for i, stage in enumerate(stages):
            if 0 <= t - i < chunks:
                stage(t - i)
    for k in range(chunks):
        c_copy(k).wait_send()
        x_copy(k).wait_send()
        gx_copy(k).wait_send()
        gc_copy(k).wait_send()
        for d in range(1, depth):
            z_copy(k, d).wait_send()
            gz_copy(k, d).wait_send()
        for m in range(4):
            for zz in range(depth):
                out_copy(k, m, zz).wait()


def on_device(gradients, local_params, first_moment, second_moment, global_params, outer_momentum):
    reps, peers = lax.axis_size("rep"), lax.axis_size("fsdp")
    depth = reps // 4
    matrices, rows, d = global_params.shape
    width = d // (CHUNKS * depth)
    f32 = jnp.float32
    piece = (rows, width)
    dma = pltpu.SemaphoreType.DMA
    block = (matrices, rows, d)
    any_spec = pl.BlockSpec(memory_space=pl.ANY)
    mean, factor = pl.pallas_call(
        functools.partial(kernel, (reps, peers, depth)),
        out_shape=(jax.ShapeDtypeStruct(block, f32), jax.ShapeDtypeStruct((8, 128), f32)),
        in_specs=[any_spec] * 4,
        out_specs=(any_spec, pl.BlockSpec(memory_space=pltpu.VMEM)),
        scratch_shapes=[
            pltpu.VMEM(block, gradients.dtype), pltpu.VMEM(block, f32), pltpu.VMEM(block, f32), pltpu.VMEM(block, f32),
            pltpu.VMEM((CHUNKS, 4, depth) + piece, f32),
            pltpu.VMEM((CHUNKS, 2, depth) + piece, f32),
            pltpu.VMEM((CHUNKS, depth) + piece, f32),
            pltpu.VMEM((CHUNKS, depth) + piece, f32),
            pltpu.VMEM((CHUNKS, depth) + piece, f32),
            pltpu.VMEM((CHUNKS, depth) + piece, f32),
            pltpu.VMEM((CHUNKS, 4, depth) + piece, f32),
            pltpu.VMEM((peers, 8, 128), f32),
            dma((4,)), dma((peers,)), dma((peers,)),
            dma((CHUNKS,)), dma((CHUNKS,)), dma((CHUNKS,)), dma((CHUNKS,)),
            dma((CHUNKS, depth)), dma((CHUNKS, depth)), dma((CHUNKS, depth)), dma((CHUNKS, depth)),
            dma((CHUNKS,)), dma((CHUNKS,)), dma((CHUNKS,)), dma((CHUNKS,)),
            dma((CHUNKS, 4, depth)),
        ],
        compiler_params=pltpu.CompilerParams(
            collective_id=0, has_side_effects=True, vmem_limit_bytes=40 * 1024 * 1024),
    )(gradients.reshape(block), local_params.reshape(block), first_moment.reshape(block), second_moment.reshape(block))
    clipped = gradients.astype(f32) * factor[0, 0]
    first_new = 0.9 * first_moment + 0.1 * clipped
    second_new = 0.95 * second_moment + 0.05 * clipped * clipped
    pseudo = global_params - mean
    momentum_next = 0.9 * outer_momentum + pseudo
    global_next = global_params - 0.7 * (pseudo + 0.9 * momentum_next)
    return (global_next, momentum_next, first_new, second_new)


def solution(mesh):
    placed = (
        P("rep", None, "fsdp", None),
        P("rep", None, "fsdp", None),
        P("rep", None, "fsdp", None),
        P("rep", None, "fsdp", None),
        P(None, "fsdp", None),
        P(None, "fsdp", None),
    )
    return jax.shard_map(
        on_device,
        mesh=mesh,
        in_specs=placed,
        out_specs=(
            P(None, "fsdp", None),
            P(None, "fsdp", None),
            P("rep", None, "fsdp", None),
            P("rep", None, "fsdp", None),
        ),
        check_vma=False,
    )
```

time: 140 us -> 61.4 us (0.44); the launches traced: 138 us -> 61.2 us
  waiting for transfers between devices: 96.1 us -> 0 us
  Pallas kernels: 0 us -> 47.8 us
  other arithmetic: 22.2 us -> 6.15 us
  between operations: 14.8 us -> 0.66 us
  local copies, waits for them, and re-layouts: 0.02 us -> 6.58 us
  blocking collectives: 4.98 us -> 0 us
    psum x1 -> x0, waiting for transfers between devices: 96.1 us -> none  [outer_step(): pseudo = lax.psum(delta, 'rep') / replicas]
    pallas_call x0 -> x1, Pallas kernels: none -> 47.8 us  [on_device(): pl.pallas_call(functools.partial(kernel, (reps, peers, depth)), out_shape...]
    sub x3 -> x1, other arithmetic: 10.2 us -> 2.66 us  [on_device(): global_next = global_params - 0.7 * (pseudo + 0.9 * momentum_next)]
    unnamed x6 -> x12, local copies, waits for them, and re-layouts: 0.02 us -> 6 us
    psum x1 -> x0, blocking collectives: 4.98 us -> none  [on_device(): squares = lax.psum(jnp.sum(gradient * gradient), 'fsdp')]
    broadcast_in_dim x1 -> x0, other arithmetic: 4.24 us -> none  [on_device(): jnp.stack(firsts)[None]]
    add x0 -> x1, other arithmetic: none -> 3.49 us  [on_device(): second_new = 0.95 * second_moment + 0.05 * clipped * clipped]
    convert_element_type x1 -> x0, other arithmetic: 2.76 us -> none  [on_device(): gradient = gradients[0].astype(jnp.float32)]
  transfers between devices with their start and end apart: 1 -> 0, of which waited for: 1 -> 0; matrix products, arithmetic and copies ran while one was open for 3% -> 0% of each run, Pallas kernels for 0% -> 0%
where the time goes in v1:
time: 61.4 us; the launch traced here: 61.2 us
  Pallas kernels  47.8 us (78%)
  local copies, waits for them, and re-layouts  6.58 us (11%)
  other arithmetic  6.15 us (10%)
  between operations  0.66 us (1%)
    pallas_call x1, Pallas kernels, on_device(): pl.pallas_call(functools.partial(kernel, (reps, peers, depth)), out_shape...  47.8 us
    unnamed x12, local copies, waits for them, and re-layouts  6 us
    add x1, other arithmetic, on_device(): second_new = 0.95 * second_moment + 0.05 * clipped * clipped  3.49 us
    sub x1, other arithmetic, on_device(): global_next = global_params - 0.7 * (pseudo + 0.9 * momentum_next)  2.66 us

profile of v1, /device:TPU:1, one launch (start us, length us, event | category | flops | bytes accessed | tf_op | source)
XLA Modules:
  0.0 61.2 jit_solution(11138226406838816172)
XLA Ops:
  0.6 0.0 copy-start
  0.6 1.6 %copy-done = f32[1,4,32,4096]{3,2,1,0:T(8,128)S(1)} copy-done((f32[1,4,32,4096]{3,2,1,0:T(8,128)S(1)}, f32[1,4,32,4096]{3,2,1,0:T(8,128)}, u32[]{:S(2)}) %copy-start) | copy-done | bytes 2097176
  2.2 0.0 copy-start.1
  2.2 1.6 %copy-done.1 = f32[1,4,32,4096]{3,2,1,0:T(8,128)S(1)} copy-done((f32[1,4,32,4096]{3,2,1,0:T(8,128)S(1)}, f32[1,4,32,4096]{3,2,1,0:T(8,128)}, u32[]{:S(2)}) %copy-start.1) | copy-done | bytes 2097176
  3.8 0.0 copy-start.2
  3.8 1.2 %copy-done.2 = bf16[1,4,32,4096]{3,2,1,0:T(8,128)(2,1)S(1)} copy-done((bf16[1,4,32,4096]{3,2,1,0:T(8,128)(2,1)S(1)}, bf16[1,4,32,4096]{3,2,1,0:T(8,128)(2,1)}, u32[]{:S(2)}) %copy-start.2) | copy-done | bytes 1048600
  5.0 0.0 copy-start.3
  5.0 1.6 %copy-done.3 = f32[1,4,32,4096]{3,2,1,0:T(8,128)S(1)} copy-done((f32[1,4,32,4096]{3,2,1,0:T(8,128)S(1)}, f32[1,4,32,4096]{3,2,1,0:T(8,128)}, u32[]{:S(2)}) %copy-start.3) | copy-done | bytes 2097176
  6.6 0.0 copy-start.4
  6.6 0.0 copy-start.5
  6.6 47.8 %shard_map.93 = (f32[4,32,4096]{2,1,0:T(8,128)S(1)}, f32[8,128]{1,0:T(8,128)S(1)}) custom-call(bf16[4,32,4096]{2,1,0:T(8,128)(2,1)S(1)} %bitcast.7, f32[4,32,4096]{2,1,0:T(8,128)S(1)} %bitcast.8, f32[4,32,4096]{2,1,0:T(8,128)S(1)} %bitcast.5, f32[4,32,4096]{2,1,0:T(8,128)S(1)} %bitcast.6), custom_call_target="tpu_custom_call" | custom-call | tf_op jit(solution)/shard_map/pallas_call | solution.py:205
  54.4 0.6 slice.3
  55.0 0.0 copy-done.4
  55.0 0.0 copy-done.5
  55.0 2.7 %multiply_subtract_fusion = (f32[4,32,4096]{2,1,0:T(8,128)}, f32[4,32,4096]{2,1,0:T(8,128)}) fusion(f32[4,32,4096]{2,1,0:T(8,128)S(1)} %copy-done.4, f32[4,32,4096]{2,1,0:T(8,128)S(1)} %copy-done.5, f32[4,32,4096]{2,1,0:T(8,128)S(1)} %get-tuple-element.6), kind=kLoop, calls=%fused_computation.4 | loop fusion | flops 3670016 | bytes 10485760 | tf_op jit(solution)/shard_map/sub | solution.py:234
  57.7 3.5 %fusion = (f32[1,4,32,4096]{3,2,1,0:T(8,128)}, f32[1,4,32,4096]{3,2,1,0:T(8,128)}) fusion(f32[1,4,32,4096]{3,2,1,0:T(8,128)S(1)} %copy-done.1, bf16[1,4,32,4096]{3,2,1,0:T(8,128)(2,1)S(1)} %copy-done.2, f32[]{:T(128)} %bitcast.4, f32[1,4,32,4096]{3,2,1,0:T(8,128)S(1)} %copy-done), kind=kLoop, calls=%fused_computation.1 | loop fusion | flops 4718592 | bytes 9437188 | tf_op jit(solution)/shard_map/add | solution.py:231
Async XLA Ops:
  0.6 1.6 %copy-start = (f32[1,4,32,4096]{3,2,1,0:T(8,128)S(1)}, f32[1,4,32,4096]{3,2,1,0:T(8,128)}, u32[]{:S(2)}) copy-start(f32[1,4,32,4096]{3,2,1,0:T(8,128)} %param.8) | copy-start | bytes 6291460
  2.2 1.6 %copy-start.1 = (f32[1,4,32,4096]{3,2,1,0:T(8,128)S(1)}, f32[1,4,32,4096]{3,2,1,0:T(8,128)}, u32[]{:S(2)}) copy-start(f32[1,4,32,4096]{3,2,1,0:T(8,128)} %param.9) | copy-start | bytes 6291460
  3.8 1.2 %copy-start.2 = (bf16[1,4,32,4096]{3,2,1,0:T(8,128)(2,1)S(1)}, bf16[1,4,32,4096]{3,2,1,0:T(8,128)(2,1)}, u32[]{:S(2)}) copy-start(bf16[1,4,32,4096]{3,2,1,0:T(8,128)(2,1)} %param.6) | copy-start | bytes 3145732
  5.0 1.6 %copy-start.3 = (f32[1,4,32,4096]{3,2,1,0:T(8,128)S(1)}, f32[1,4,32,4096]{3,2,1,0:T(8,128)}, u32[]{:S(2)}) copy-start(f32[1,4,32,4096]{3,2,1,0:T(8,128)} %param.7) | copy-start | bytes 6291460
  6.6 48.4 %copy-start.4 = (f32[4,32,4096]{2,1,0:T(8,128)S(1)}, f32[4,32,4096]{2,1,0:T(8,128)}, u32[]{:S(2)}) copy-start(f32[4,32,4096]{2,1,0:T(8,128)} %param.10) | copy-start | bytes 6291460
  6.6 48.4 %copy-start.5 = (f32[4,32,4096]{2,1,0:T(8,128)S(1)}, f32[4,32,4096]{2,1,0:T(8,128)}, u32[]{:S(2)}) copy-start(f32[4,32,4096]{2,1,0:T(8,128)} %param.11) | copy-start | bytes 6291460

commit v2 on v1

--- a/solution.py
+++ b/solution.py
@@ -14,8 +14,8 @@
 MESH = pl.DeviceIdType.MESH
 
 
-def kernel(shape, g_hbm, p_hbm, f_hbm, s_hbm, mean_hbm, factor_ref,
-           g, p, f, s, delta, recv_c, part_x, recv_x, part_z, recv_z, res, squares,
+def kernel(shape, g_hbm, p_hbm, f_hbm, s_hbm, w_hbm, v_hbm, new_w, new_v, new_f, new_s,
+           g, p, f, s, w, v, delta, recv_c, part_x, recv_x, part_z, recv_z, res, squares,
            load_sem, sq_send, sq_recv, c_send, c_recv, x_send, x_recv, z_send, z_recv,
            gz_send, gz_recv, gx_send, gx_recv, gc_send, gc_recv, out_sem):
     reps, peers, depth = shape
@@ -36,7 +36,7 @@
     mine_id = lax.rem(me, 4)
 
     loads = [pltpu.make_async_copy(src, dst, load_sem.at[i])
-             for i, (src, dst) in enumerate(((g_hbm, g), (f_hbm, f), (s_hbm, s), (p_hbm, p)))]
+             for i, (src, dst) in enumerate(((g_hbm, g), (f_hbm, f), (s_hbm, s), (p_hbm, p), (w_hbm, w), (v_hbm, v)))]
     for load in loads:
         load.start()
 
@@ -75,8 +75,7 @@
         total = total + squares[d]
     mean_sq = jnp.sum(total, keepdims=True) / (g.shape[0] * rows * g.shape[2] * peers)
     factor = jnp.where(mean_sq > 0.25, 0.5 / jnp.sqrt(mean_sq), 1.0)
-    factor_ref[...] = jnp.broadcast_to(factor, factor_ref.shape)
-    for load in loads[1:]:
+    for load in loads[1:4]:
         load.wait()
 
     def columns(k, zz):
@@ -90,6 +89,8 @@
             clipped = g[m, :, at].astype(jnp.float32) * factor
             first = 0.9 * f[m, :, at] + 0.1 * clipped
             second = 0.95 * s[m, :, at] + 0.05 * clipped * clipped
+            f[m, :, at] = first
+            s[m, :, at] = second
             update = (first * (0.1 / FIRST_FIX)) / (jnp.sqrt(second * (1.0 / SECOND_FIX)) + 1e-8)
             delta[k, m, zz] = 0.99 * p[m, :, at] - update
             return 0
@@ -117,8 +118,13 @@
         own = res.at[k, pl.ds(2 * core, 2)]
         return remote(own, own, gc_send.at[k], gc_recv.at[k], other_core)
 
-    def out_copy(k, m, zz):
-        return pltpu.make_async_copy(res.at[k, m, zz], mean_hbm.at[m, :, columns(k, zz)], out_sem.at[k, m, zz])
+    def out_copies(k):
+        at = pl.ds(k * depth * width, depth * width)
+        return [pltpu.make_async_copy(src.at[:, :, at], dst.at[:, :, at], out_sem.at[i, k])
+                for i, (src, dst) in enumerate(((w, new_w), (v, new_v)))]
+
+    moments = [pltpu.make_async_copy(src, dst, load_sem.at[i])
+               for i, (src, dst) in enumerate(((f, new_f), (s, new_s)))]
 
     def compute(k):
         half(k, 1 - core)
@@ -165,15 +171,30 @@
 
     def gather_core(k):
         gc_copy(k).wait_recv()
-        for m in range(4):
-            for zz in range(depth):
-                out_copy(k, m, zz).start()
+
+        def piece(i, _):
+            m = i // depth
+            zz = lax.rem(i, depth)
+            at = columns(k, zz)
+            now = w[m, :, at]
+            pseudo = now - res[k, m, zz]
+            momentum = 0.9 * v[m, :, at] + pseudo
+            v[m, :, at] = momentum
+            w[m, :, at] = now - 0.7 * (pseudo + 0.9 * momentum)
+            return 0
+        lax.fori_loop(0, 4 * depth, piece, 0)
+        for copy in out_copies(k):
+            copy.start()
 
     for k in range(chunks):
         compute(k)
         if k:
             reduce_core(k - 1)
     reduce_core(chunks - 1)
+    for copy in moments:
+        copy.start()
+    for load in loads[4:]:
+        load.wait()
     stages = (reduce_x, reduce_z, gather_z, gather_x, gather_core)
     for t in range(chunks + len(stages) - 1):
         for i, stage in enumerate(stages):
@@ -187,9 +208,10 @@
         for d in range(1, depth):
             z_copy(k, d).wait_send()
             gz_copy(k, d).wait_send()
-        for m in range(4):
-            for zz in range(depth):
-                out_copy(k, m, zz).wait()
+        for copy in out_copies(k):
+            copy.wait()
+    for copy in moments:
+        copy.wait()
 
 
 def on_device(gradients, local_params, first_moment, second_moment, global_params, outer_momentum):
@@ -201,14 +223,13 @@
     piece = (rows, width)
     dma = pltpu.SemaphoreType.DMA
     block = (matrices, rows, d)
-    any_spec = pl.BlockSpec(memory_space=pl.ANY)
-    mean, factor = pl.pallas_call(
+    outs = pl.pallas_call(
         functools.partial(kernel, (reps, peers, depth)),
-        out_shape=(jax.ShapeDtypeStruct(block, f32), jax.ShapeDtypeStruct((8, 128), f32)),
-        in_specs=[any_spec] * 4,
-        out_specs=(any_spec, pl.BlockSpec(memory_space=pltpu.VMEM)),
+        out_shape=(jax.ShapeDtypeStruct(block, f32),) * 4,
+        in_specs=[pl.BlockSpec(memory_space=pltpu.HBM)] * 6,
+        out_specs=(pl.BlockSpec(memory_space=pl.ANY),) * 4,
         scratch_shapes=[
-            pltpu.VMEM(block, gradients.dtype), pltpu.VMEM(block, f32), pltpu.VMEM(block, f32), pltpu.VMEM(block, f32),
+            pltpu.VMEM(block, gradients.dtype), *[pltpu.VMEM(block, f32)] * 5,
             pltpu.VMEM((CHUNKS, 4, depth) + piece, f32),
             pltpu.VMEM((CHUNKS, 2, depth) + piece, f32),
             pltpu.VMEM((CHUNKS, depth) + piece, f32),
@@ -217,22 +238,17 @@
             pltpu.VMEM((CHUNKS, depth) + piece, f32),
             pltpu.VMEM((CHUNKS, 4, depth) + piece, f32),
             pltpu.VMEM((peers, 8, 128), f32),
-            dma((4,)), dma((peers,)), dma((peers,)),
+            dma((6,)), dma((peers,)), dma((peers,)),
             dma((CHUNKS,)), dma((CHUNKS,)), dma((CHUNKS,)), dma((CHUNKS,)),
             dma((CHUNKS, depth)), dma((CHUNKS, depth)), dma((CHUNKS, depth)), dma((CHUNKS, depth)),
             dma((CHUNKS,)), dma((CHUNKS,)), dma((CHUNKS,)), dma((CHUNKS,)),
-            dma((CHUNKS, 4, depth)),
+            dma((2, CHUNKS)),
         ],
         compiler_params=pltpu.CompilerParams(
-            collective_id=0, has_side_effects=True, vmem_limit_bytes=40 * 1024 * 1024),
-    )(gradients.reshape(block), local_params.reshape(block), first_moment.reshape(block), second_moment.reshape(block))
-    clipped = gradients.astype(f32) * factor[0, 0]
-    first_new = 0.9 * first_moment + 0.1 * clipped
-    second_new = 0.95 * second_moment + 0.05 * clipped * clipped
-    pseudo = global_params - mean
-    momentum_next = 0.9 * outer_momentum + pseudo
-    global_next = global_params - 0.7 * (pseudo + 0.9 * momentum_next)
-    return (global_next, momentum_next, first_new, second_new)
+            collective_id=0, has_side_effects=True, vmem_limit_bytes=28 * 1024 * 1024),
+    )(*[pltpu.with_memory_space_constraint(a.reshape(block), pltpu.HBM)
+        for a in (gradients, local_params, first_moment, second_moment, global_params, outer_momentum)])
+    return (outs[0], outs[1], outs[2][None], outs[3][None])
 
 
 def solution(mesh):

time: 61.4 us -> 53.1 us (0.86)
  other arithmetic: 6.15 us -> 0 us
  local copies, waits for them, and re-layouts: 6.58 us -> 5.28 us
  Pallas kernels: 47.8 us -> 47 us
    add x1 -> x0, other arithmetic: 3.49 us -> none  [on_device(): second_new = 0.95 * second_moment + 0.05 * clipped * clipped]
    sub x1 -> x0, other arithmetic: 2.66 us -> none  [on_device(): global_next = global_params - 0.7 * (pseudo + 0.9 * momentum_next)]
    pallas_call x1, Pallas kernels: 47.8 us -> 47 us  [on_device(): pl.pallas_call(functools.partial(kernel, (reps, peers, depth)), out_shape...]
    unnamed x12 -> x4, local copies, waits for them, and re-layouts: 6 us -> 5.28 us
where the time goes in v2:
time: 53.1 us; the launch traced here: 52.9 us
  Pallas kernels  47 us (89%)
  local copies, waits for them, and re-layouts  5.28 us (10%)
  between operations  0.64 us (1%)
    pallas_call x1, Pallas kernels, on_device(): pl.pallas_call(functools.partial(kernel, (reps, peers, depth)), out_shape...  47 us
    unnamed x4, local copies, waits for them, and re-layouts  5.28 us

profile of v2, /device:TPU:1, one launch (start us, length us, event | category | flops | bytes accessed | tf_op | source)
XLA Modules:
  0.0 52.9 jit_solution(2633218933385547447)
XLA Ops:
  0.6 47.0 %shard_map.93 = (f32[4,32,4096]{2,1,0:T(8,128)S(1)}, f32[4,32,4096]{2,1,0:T(8,128)S(1)}, f32[4,32,4096]{2,1,0:T(8,128)S(1)}, f32[4,32,4096]{2,1,0:T(8,128)S(1)}) custom-call(bf16[4,32,4096]{2,1,0:T(8,128)(2,1)} %bitcast.11, f32[4,32,4096]{2,1,0:T(8,128)} %bitcast.8, f32[4,32,4096]{2,1,0:T(8,128)} %bitcast.9, f32[4,32,4096]{2,1,0:T(8,128)} %bitcast.10, ...), custom_call_target="tpu_custom_call" | custom-call | tf_op jit(solution)/shard_map/pallas_call | solution.py:226
  47.6 1.3 %copy.14 = f32[4,32,4096]{2,1,0:T(8,128)} copy(f32[4,32,4096]{2,1,0:T(8,128)S(1)} %get-tuple-element.16) | data formatting | bytes 4194304
  48.9 1.3 %copy.15 = f32[4,32,4096]{2,1,0:T(8,128)} copy(f32[4,32,4096]{2,1,0:T(8,128)S(1)} %get-tuple-element.17) | data formatting | bytes 4194304
  50.3 1.3 %copy.16 = f32[1,4,32,4096]{3,2,1,0:T(8,128)} copy(f32[1,4,32,4096]{3,2,1,0:T(8,128)S(1)} %bitcast.7) | data formatting | bytes 4194304
  51.6 1.3 %copy.17 = f32[1,4,32,4096]{3,2,1,0:T(8,128)} copy(f32[1,4,32,4096]{3,2,1,0:T(8,128)S(1)} %bitcast.6) | data formatting | bytes 4194304
